TPU v7x, 32 devices: a whole 2x2x4 slice. The times are simulated.
32 devices in a mesh: seq: 8 (over y, x, core), sub: 4 (over z).
Axes of the slice: x: 2, y: 2, z: 4, core: 2. Of those that a mesh axis runs over, the one named last changes fastest.
Arguments:
- query_rows: bfloat16 [8192, 1120], P(('seq', 'sub')), may hold values from -6 to 6
- key_rows: bfloat16 [8192, 1120], P(('seq', 'sub')), may hold values from -6 to 6
- value_rows: bfloat16 [8192, 1120], P(('seq', 'sub')), may hold values from -6 to 6
- query_tangent: bfloat16 [8192, 1120], P(('seq', 'sub')), may hold values from -6 to 6
- key_tangent: bfloat16 [8192, 1120], P(('seq', 'sub')), may hold values from -6 to 6
- value_tangent: bfloat16 [8192, 1120], P(('seq', 'sub')), may hold values from -6 to 6
- teacher: bfloat16 [8192, 2240], P(('seq', 'sub')), may hold values from -64 to 64
- out_weight: bfloat16 [1120, 2240], replicated, may hold values from -0.1875 to 0.1875
- norm_gain: float32 [1120], replicated, may hold values from 0.1 to 1.9
- clip_length: int32 [1], replicated, may hold values from 4096 to 8192
- block_mask: int32 [128], P(('seq', 'sub')), may hold values 0 or 1
Outputs:
- residual: bfloat16 [8192, 2240], P(('seq', 'sub'))
- grad_query: bfloat16 [8192, 1120], P(('seq', 'sub'))
- grad_key: bfloat16 [8192, 1120], P(('seq', 'sub'))
- grad_value: bfloat16 [8192, 1120], P(('seq', 'sub'))
All inputs are finite; a program needn't handle non-finite values. No bound on the sum of `block_mask` on one device may be relied on, other than what follows from the above.
Results may differ from a plain program's by a relative error of at most 0.007.
Values may be sent and summed in bfloat16 or wider, within the bound.
A program may use at most 64 MiB of HBM per device.

v0:
```python
import jax
import jax.numpy as jnp
from jax import lax
from jax.sharding import PartitionSpec as P

H = 10
E = 112
BLK = 64


def split_heads(matrix):
    return matrix.reshape(matrix.shape[0], H, E)


def norm_back(unnorm, scale_inv, weighted):
    inner_mean = jnp.mean(unnorm * weighted, axis=-1, keepdims=True)
    return scale_inv * weighted - unnorm * (scale_inv * scale_inv * scale_inv) * inner_mean


def combine_states(stacked):
    totals = lax.psum(stacked, ("seq", "sub"))
    return totals.astype(jnp.bfloat16)


def local(
    query_rows,
    key_rows,
    value_rows,
    query_tangent,
    key_tangent,
    value_tangent,
    teacher,
    out_weight,
    norm_gain,
    clip_length,
    block_mask,
):
    f32 = jnp.float32
    bf16 = jnp.bfloat16
    tok_rows = query_rows.shape[0]
    first_row = (lax.axis_index("seq") * lax.axis_size("sub") + lax.axis_index("sub")) * tok_rows
    position = first_row + lax.iota(jnp.int32, tok_rows)
    block_flags = jnp.broadcast_to(block_mask[:, None], (tok_rows // BLK, BLK)).reshape(tok_rows)
    valid_rows = jnp.where((position < clip_length[0]) & (block_flags == 1), 1.0, 0.0).astype(f32)[
        :, None
    ]
    key_vals = key_rows.astype(f32)
    key_feat = (valid_rows * jnp.maximum(key_vals, 0.0)).astype(bf16)
    key_slope = valid_rows * jnp.where(key_vals > 0, 1.0, 0.0).astype(f32)
    key_dot = (key_slope * key_tangent.astype(f32)).astype(bf16)
    value_heads = split_heads(value_rows)
    feat_keys = split_heads(key_feat)
    state_part = jnp.einsum("the,thf->hef", feat_keys, value_heads, preferred_element_type=f32)
    tangent_part = jnp.einsum(
        "the,thf->hef", split_heads(key_dot), value_heads, preferred_element_type=f32
    ) + jnp.einsum(
        "the,thf->hef", feat_keys, split_heads(value_tangent), preferred_element_type=f32
    )
    states = combine_states(jnp.stack([state_part, tangent_part]))
    state = states[0]
    state_dot = states[1]
    query_vals = query_rows.astype(f32)
    query_feat = jnp.maximum(query_vals, 0.0).astype(bf16)
    query_slope = jnp.where(query_vals > 0, 1.0, 0.0).astype(f32)
    query_dot = (query_slope * query_tangent.astype(f32)).astype(bf16)
    feat_heads = split_heads(query_feat)
    unnorm = jnp.einsum("the,hef->thf", feat_heads, state, preferred_element_type=f32)
    unnorm_dot = jnp.einsum(
        "the,hef->thf", split_heads(query_dot), state, preferred_element_type=f32
    ) + jnp.einsum("the,hef->thf", feat_heads, state_dot, preferred_element_type=f32)
    gain_heads = norm_gain.reshape(H, E)
    scale_inv = lax.rsqrt(jnp.mean(unnorm * unnorm, axis=-1, keepdims=True) + 1e-06)
    normed_dot = (
        (gain_heads * norm_back(unnorm, scale_inv, unnorm_dot))
        .astype(bf16)
        .reshape(tok_rows, H * E)
    )
    velocity = jnp.dot(normed_dot, out_weight, preferred_element_type=f32)
    residual = (velocity - teacher.astype(f32)).astype(bf16)
    normed_grad = lax.dot_general(
        residual, out_weight, (((1,), (1,)), ((), ())), preferred_element_type=f32
    )
    unnorm_grad = norm_back(unnorm, scale_inv, gain_heads * split_heads(normed_grad)).astype(bf16)
    grad_part = jnp.einsum("the,thf->hef", feat_heads, unnorm_grad, preferred_element_type=f32)
    state_grad = combine_states(grad_part[None])[0]
    grad_query = (
        query_slope
        * jnp.einsum("thf,hef->the", unnorm_grad, state, preferred_element_type=f32).reshape(
            tok_rows, H * E
        )
    ).astype(bf16)
    grad_key = (
        key_slope
        * jnp.einsum("thf,hef->the", value_heads, state_grad, preferred_element_type=f32).reshape(
            tok_rows, H * E
        )
    ).astype(bf16)
    grad_value = (
        jnp.einsum("the,hef->thf", feat_keys, state_grad, preferred_element_type=f32)
        .reshape(tok_rows, H * E)
        .astype(bf16)
    )
    return (residual, grad_query, grad_key, grad_value)


def solution(mesh):
    return jax.shard_map(
        local,
        mesh=mesh,
        in_specs=(
            P(("seq", "sub"), None),
            P(("seq", "sub"), None),
            P(("seq", "sub"), None),
            P(("seq", "sub"), None),
            P(("seq", "sub"), None),
            P(("seq", "sub"), None),
            P(("seq", "sub"), None),
            P(),
            P(),
            P(),
            P(("seq", "sub")),
        ),
        out_specs=(
            P(("seq", "sub"), None),
            P(("seq", "sub"), None),
            P(("seq", "sub"), None),
            P(("seq", "sub"), None),
        ),
        check_vma=False,
    )
```

profile of v0, /device:TPU:0, one launch (start us, length us, event | category | flops | bytes accessed | tf_op | source)
XLA Modules:
  0.0 119.9 jit_solution(6810560053801250112)
XLA Ops:
  1.4 0.4 copy-done
  1.7 0.7 broadcast_compare_fusion
  2.5 0.8 mul.117
  3.3 1.6 %fusion.4 = (bf16[256,1120]{0,1:T(8,128)(2,1)S(1)}, bf16[256,1120]{0,1:T(8,128)(2,1)S(1)}) fusion(bf16[256,1120]{0,1:T(8,128)(2,1)} %param.12, f32[256]{0:T(256)S(1)} %and_select_fusion, bf16[256,1120]{0,1:T(8,128)(2,1)} %param.15), kind=kLoop, calls=%fused_computation.17 | loop fusion | flops 2867200 | bytes 2294784 | tf_op jit(solution)/shard_map/convert_element_type | solution.py:48
  5.3 0.7 copy-done.3
  6.0 0.3 fusion.2
  6.3 0.3 convolution_bitcast_fusion.2
  6.7 53.7 %all-reduce.2 = bf16[2,10,112,112]{3,2,1,0:T(8,128)(2,1)S(1)} all-reduce(f32[2,10,112,112]{3,2,1,0:T(8,128)S(1)} %pad_maximum_fusion), channel_id=1, replica_groups=mesh['seq'=8,'sub'=4] {'seq','sub'}, use_global_device_ids=true, to_apply=%region_0.1 | all-reduce | flops 250880 | bytes 1505280 | tf_op jit(solution)/shard_map/psum | solution.py:21
  60.5 1.5 %fusion.5 = (bf16[256,1120]{0,1:T(8,128)(2,1)S(1)}, bf16[256,1120]{0,1:T(8,128)(2,1)S(1)}) fusion(bf16[256,1120]{0,1:T(8,128)(2,1)S(1)} %copy-done.1, bf16[256,1120]{0,1:T(8,128)(2,1)} %param.14), kind=kLoop, calls=%fused_computation.18 | loop fusion | flops 2293760 | bytes 2293760 | tf_op jit(solution)/shard_map/convert_element_type | solution.py:63
  61.9 0.4 fusion.13
  62.3 0.4 fusion.1
  62.7 0.4 multiply_reduce_fusion.2
  63.1 0.6 multiply_convert_fusion
  63.7 0.7 copy-done.4
  64.5 2.3 %fusion = bf16[256,2240]{0,1:T(8,128)(2,1)S(1)} fusion(bf16[256,1120]{0,1:T(8,128)(2,1)S(1)} %bitcast.81, bf16[1120,2240]{1,0:T(8,128)(2,1)S(1)} %bitcast.83, bf16[256,2240]{0,1:T(8,128)(2,1)S(1)} %copy-done.4), kind=kOutput, calls=%fused_computation.1 | convolution fusion | flops 1286225920 | bytes 7884800 | tf_op jit(solution)/shard_map/dot_general | solution.py:78
  66.8 1.5 %fusion.17 = f32[256,1120]{0,1:T(8,128)S(1)} fusion(bf16[1120,2240]{1,0:T(8,128)(2,1)S(1)} %bitcast.83, bf16[256,2240]{0,1:T(8,128)(2,1)S(1)} %fusion), kind=kOutput, calls=%fused_computation.47 | convolution fusion | flops 1284505600 | bytes 7311360 | tf_op jit(solution)/shard_map/dot_general | solution.py:80
  68.6 0.3 subtract_convert_fusion
  68.9 0.3 convolution_bitcast_fusion.1
  69.2 0.3 fusion.12
  69.5 1.0 fusion.7
  70.5 46.1 %all-reduce.3 = bf16[1,10,112,112]{3,2,1,0:T(8,128)(2,1)S(1)} all-reduce(f32[1,10,112,112]{3,2,1,0:T(8,128)S(1)} %convolution_bitcast_fusion.1), channel_id=1, replica_groups=mesh['seq'=8,'sub'=4] {'seq','sub'}, use_global_device_ids=true, to_apply=%region_4.5 | all-reduce | flops 125440 | bytes 752640 | tf_op jit(solution)/shard_map/psum | solution.py:21
  116.6 1.2 convolution_convert_fusion
  118.1 0.8 copy-done.2
  118.9 1.0 fusion.8
  (22 shorter events, 1.1 us)
Async XLA Ops:
  0.6 1.1 copy-start
  4.9 1.1 copy-start.3
  6.7 53.7 %copy-start.1 = (bf16[256,1120]{0,1:T(8,128)(2,1)S(1)}, bf16[256,1120]{0,1:T(8,128)(2,1)}, u32[]{:S(2)}) copy-start(bf16[256,1120]{0,1:T(8,128)(2,1)} %param.11) | copy-start | bytes 1720324
  60.5 3.3 %slice-start = ((s8[5160960]{0:T(1024)(128)(4,1)}), s8[4194304]{0:T(1024)(128)(4,1)S(1)}, s32[]{:S(2)}) async-start(s8[5160960]{0:T(1024)(128)(4,1)} %bitcast.82), calls=%async_computation | async-start | bytes 8388608
  62.3 1.4 %slice-start.1 = ((s8[5160960]{0:T(1024)(128)(4,1)}), s8[966656]{0:T(1024)(128)(4,1)S(1)}, s32[]{:S(2)}) async-start(s8[5160960]{0:T(1024)(128)(4,1)} %bitcast.82), calls=%async_computation.1 | async-start | bytes 1933312
  63.1 1.3 %copy-start.4 = (bf16[256,2240]{0,1:T(8,128)(2,1)S(1)}, bf16[256,2240]{0,1:T(8,128)(2,1)}, u32[]{:S(2)}) copy-start(bf16[256,2240]{0,1:T(8,128)(2,1)} %param.17) | copy-start | bytes 3440644
  66.8 1.5 %copy-start.5 = (bf16[256,2240]{0,1:T(8,128)(2,1)}, bf16[256,2240]{0,1:T(8,128)(2,1)S(1)}, u32[]{:S(2)}) copy-start(bf16[256,2240]{0,1:T(8,128)(2,1)S(1)} %fusion) | copy-start | bytes 3440644
  117.8 1.1 copy-start.2
where the time goes:
time: 120 us
  blocking collectives  99.8 us (83%)
  matrix products  7.92 us (7%)
  other arithmetic  7.01 us (6%)
  local copies, waits for them, and re-layouts  3.56 us (3%)
  between operations  1.56 us (1%)
    psum x2, blocking collectives, combine_states(): totals = lax.psum(stacked, ('seq', 'sub'))  99.8 us
    unnamed x16, local copies, waits for them, and re-layouts  2.62 us

commit v1 on v0

--- a/solution.py
+++ b/solution.py
@@ -18,7 +18,7 @@
 
 
 def combine_states(stacked):
-    totals = lax.psum(stacked, ("seq", "sub"))
+    totals = lax.psum(lax.psum(stacked, "sub"), "seq")
     return totals.astype(jnp.bfloat16)
 
 

time: 120 us -> 214 us (1.78)
  waiting for transfers between devices: 0 us -> 91 us
  blocking collectives: 99.8 us -> 83.6 us
  between operations: 1.56 us -> 15 us
  matrix products: 7.92 us -> 12.5 us
    psum x0 -> x2, waiting for transfers between devices: none -> 90.9 us  [combine_states(): totals = lax.psum(lax.psum(stacked, 'sub'), 'seq')]
    psum x2, blocking collectives: 99.8 us -> 83.6 us  [combine_states(): totals = lax.psum(lax.psum(stacked, 'sub'), 'seq')]
    dot_general x1, matrix products: 2.33 us -> 5.09 us  [local(): velocity = jnp.dot(normed_dot, out_weight, preferred_element_type=f32)]
  transfers between devices with their start and end apart: 0 -> 2, of which waited for: 0 -> 2; matrix products, arithmetic and copies ran while one was open for 0% -> 1% of each run, Pallas kernels for 0% -> 0%
where the time goes in v1:
time: 214 us; the launch traced here: 213 us
  waiting for transfers between devices  91 us (43%)
  blocking collectives  83.6 us (39%)
  between operations  15 us (7%)
  matrix products  12.5 us (6%)
  other arithmetic  8.03 us (4%)
  local copies, waits for them, and re-layouts  3.14 us (1%)
    psum x2, waiting for transfers between devices, combine_states(): totals = lax.psum(lax.psum(stacked, 'sub'), 'seq')  90.9 us
    psum x2, blocking collectives, combine_states(): totals = lax.psum(lax.psum(stacked, 'sub'), 'seq')  83.6 us
    dot_general x1, matrix products, local(): velocity = jnp.dot(normed_dot, out_weight, preferred_element_type=f32)  5.09 us
  transfers between devices with their start and end apart: 2, of which 2 were waited for; matrix products, arithmetic and copies ran while one was open for 1% of the time, Pallas kernels for 0%

profile of v1, /device:TPU:0, one launch (start us, length us, event | category | flops | bytes accessed | tf_op | source)
XLA Modules:
  0.0 213.3 jit_solution(8768450780894069826)
XLA Ops:
  7.9 0.7 broadcast_compare_fusion
  8.8 1.6 fusion.4
  10.7 0.3 convolution_bitcast_fusion.2
  11.0 0.7 copy-done.3
  11.8 0.3 fusion.2
  12.1 1.1 pad_maximum_fusion
  13.3 0.9 copy-done.1
  14.4 0.3 fusion.5
  14.7 56.3 %all-reduce.5.cloned.1.call-done = f32[2,10,112,112]{3,2,1,0:T(8,128)} async-done(((f32[2,10,112,112]{3,2,1,0:T(8,128)}), f32[2,10,112,112]{3,2,1,0:T(8,128)}) %all-reduce.5.cloned.1.call-update) | async-done | bytes 1003536 | tf_op jit(solution)/shard_map/psum | solution.py:21
  71.0 52.6 %all-reduce.8 = bf16[2,10,112,112]{3,2,1,0:T(8,128)(2,1)S(1)} all-reduce(f32[2,10,112,112]{3,2,1,0:T(8,128)} %all-reduce.5.cloned.1.call-done), channel_id=1, replica_groups=mesh['seq'=8,'sub'=4] {'seq'}, use_global_device_ids=true, to_apply=%region_1.2 | all-reduce | flops 250880 | bytes 1505280 | tf_op jit(solution)/shard_map/psum | solution.py:21
  123.6 0.4 fusion.13
  124.0 0.4 fusion.1
  124.3 0.4 multiply_reduce_fusion.2
  124.8 0.5 multiply_convert_fusion
  125.6 5.1 %fusion = bf16[256,2240]{0,1:T(8,128)(2,1)S(1)} fusion(bf16[256,1120]{0,1:T(8,128)(2,1)S(1)} %bitcast.81, bf16[1120,2240]{1,0:T(8,128)(2,1)} %param.18, bf16[256,2240]{0,1:T(8,128)(2,1)S(1)} %copy-done.6), kind=kOutput, calls=%fused_computation.1 | convolution fusion | flops 1286225920 | bytes 7884800 | tf_op jit(solution)/shard_map/dot_general | solution.py:78
  130.7 1.5 fusion.17
  132.8 1.1 convolution_bitcast_fusion.1
  133.9 1.3 fusion.12
  135.3 2.3 %fusion.7 = bf16[256,1120]{0,1:T(8,128)(2,1)} fusion(f32[10,112,256]{2,1,0:T(8,128)} %fusion.12, bf16[256,1120]{0,1:T(8,128)(2,1)S(1)} %copy-done.1), kind=kLoop, calls=%fused_computation.20 | loop fusion | flops 1433600 | bytes 2293760 | tf_op jit(solution)/shard_map/convert_element_type | solution.py:91
  137.5 34.6 %all-reduce.7.cloned.1.call-done = f32[1,10,112,112]{3,2,1,0:T(8,128)} async-done(((f32[1,10,112,112]{3,2,1,0:T(8,128)}), f32[1,10,112,112]{3,2,1,0:T(8,128)}) %all-reduce.7.cloned.1.call-update) | async-done | bytes 501776 | tf_op jit(solution)/shard_map/psum | solution.py:21
  172.1 31.0 %all-reduce.9 = bf16[1,10,112,112]{3,2,1,0:T(8,128)(2,1)S(1)} all-reduce(f32[1,10,112,112]{3,2,1,0:T(8,128)} %all-reduce.7.cloned.1.call-done), channel_id=1, replica_groups=mesh['seq'=8,'sub'=4] {'seq'}, use_global_device_ids=true, to_apply=%region_6.7 | all-reduce | flops 125440 | bytes 752640 | tf_op jit(solution)/shard_map/psum | solution.py:21
  203.2 1.2 convolution_convert_fusion
  204.7 0.8 copy-done.2
  205.4 1.0 fusion.8
  (32 shorter events, 2.0 us)
Async XLA Ops:
  7.2 3.2 %copy-start = (bf16[256,1120]{0,1:T(8,128)(2,1)S(1)}, bf16[256,1120]{0,1:T(8,128)(2,1)}, u32[]{:S(2)}) copy-start(bf16[256,1120]{0,1:T(8,128)(2,1)} %param.13) | copy-start | bytes 1720324
  7.2 63.8 %all-reduce.5.cloned.1.call-start = ((), (), s32[]{:S(2)}) async-start(), calls=%async_computation | async-start | bytes 2293760 | tf_op jit(solution)/shard_map/psum | solution.py:21
  10.7 1.1 copy-start.3
  12.1 1.2 copy-start.5
  13.2 1.1 copy-start.1
  13.2 1.2 copy-start.4
  13.2 158.9 %all-reduce.7.cloned.1.call-start = ((), (), s32[]{:S(2)}) async-start(), calls=%async_computation.1 | async-start | bytes 1146880 | tf_op jit(solution)/shard_map/psum | solution.py:21
  124.3 1.3 copy-start.6
  124.8 5.9 %slice-start = ((s8[5160960]{0:T(1024)(128)(4,1)}), s8[4194304]{0:T(1024)(128)(4,1)S(1)}, s32[]{:S(2)}) async-start(s8[5160960]{0:T(1024)(128)(4,1)} %bitcast.82), calls=%async_computation.2 | async-start | bytes 8388608
  125.6 5.1 %slice-start.1 = ((s8[5160960]{0:T(1024)(128)(4,1)}), s8[966656]{0:T(1024)(128)(4,1)S(1)}, s32[]{:S(2)}) async-start(s8[5160960]{0:T(1024)(128)(4,1)} %bitcast.82), calls=%async_computation.3 | async-start | bytes 1933312
  130.7 1.5 copy-start.7
  204.4 1.1 copy-start.2
Sparse Core Ops, SparseCore 0:
  13.3 57.6 all-reduce.4
  135.4 36.7 all-reduce.6
